TPU v7x, 768 devices: a whole 4x8x12 slice. The times are simulated.
768 devices in a mesh: sec: 8 (over y_lo, core), blk: 96 (over x, y_hi, z).
Axes of the slice: x: 4, y: 8 (y_hi: 2, y_lo: 4; y = y_hi * 4 + y_lo), z: 12, core: 2. Of those that a mesh axis runs over, the one named last changes fastest.
Arguments:
- fluid_temp: float32 [8, 512, 12288], P(None, 'sec', 'blk'), may hold values from -6 to 6
- stream_velocity: float32 [8, 512, 12288], P(None, 'sec', 'blk'), may hold values from 0.2 to 1
- pitch_velocity: float32 [8, 512, 12288], P(None, 'sec', 'blk'), may hold values from -0.5 to 0.5
- film_coeff: float32 [512, 12288], P('sec', 'blk'), may hold values from 0.1 to 0.3
- solid_temp: float32 [8, 32, 12288], P('sec', None, 'blk'), may hold values from -6 to 6
- conductivity: float32 [8, 32, 12288], P('sec', None, 'blk'), may hold values from 0.5 to 2
- face_owner: int32 [8, 96, 64, 1], P('sec', 'blk'), may hold values from 0 to 95; in each aligned block of 64 rows (0 to 63, 64 to 127, ..., all dimensions but the last counted through in order) at most 2 rows name the same one
Outputs:
- fluid_out: float32 [8, 512, 12288], P(None, 'sec', 'blk')
- solid_out: float32 [8, 32, 12288], P('sec', None, 'blk')
Inputs may be any that keep to these rules, and one draw needn't show every extreme that they name: `face_owner`: the 64 wall blocks of one device name any one owner at most 2 times; some device names some owner exactly 2 times.
All inputs are finite; a program needn't handle non-finite values.
Results may differ from a plain program's by a relative error of at most 0.0001.
Values sent between devices are 32-bit elements; how exact they have to be, the bound alone decides.
A program may use at most 32 MiB of HBM per device.

v0:
```python
import jax
import jax.numpy as jnp
from jax import lax
from jax.sharding import PartitionSpec as P

SUB = 4


ADVECT = 0.4
SPREAD = 0.04
WALL = 0.4
SOLID_STEP = 0.04
COOLING = 0.5
COOLANT = -1.0


def padded(block, sides, width, periodic):
    for axis, dim in sides:
        count = lax.axis_size(axis)
        forward = [(i, i + 1) for i in range(count - 1)]
        if periodic:
            forward.append((count - 1, 0))
        backward = [(target, source) for source, target in forward]
        low = lax.ppermute(
            lax.slice_in_dim(block, block.shape[dim] - width, None, axis=dim), axis, forward
        )
        high = lax.ppermute(lax.slice_in_dim(block, 0, width, axis=dim), axis, backward)
        block = jnp.concatenate([low, block, high], axis=dim)
    return block


def fluid_update(
    fluid, stream_velocity, pitch_velocity, wall_flux, pitch_extended, stream_extended
):
    pitch_prev = pitch_extended[:, :-2]
    pitch_next = pitch_extended[:, 2:]
    stream_prev = stream_extended[:, :, :-2]
    stream_next = stream_extended[:, :, 2:]
    span_prev = jnp.concatenate([fluid[:1], fluid[:-1]], 0)
    span_next = jnp.concatenate([fluid[1:], fluid[-1:]], 0)
    spread = SPREAD * (
        pitch_prev + pitch_next + stream_prev + stream_next + span_prev + span_next - 6.0 * fluid
    )
    carried = (
        -ADVECT * stream_velocity * (fluid - stream_prev)
        - ADVECT * jnp.maximum(pitch_velocity, 0.0) * (fluid - pitch_prev)
        + ADVECT * jnp.maximum(-pitch_velocity, 0.0) * (pitch_next - fluid)
    )
    updated = fluid + spread + carried
    return updated.at[0].add(-WALL * wall_flux)


def solid_update(solid, conduct, inflow, solid_extended, conduct_extended):
    stream_prev = solid_extended[..., :-2]
    stream_next = solid_extended[..., 2:]
    conduct_prev = conduct_extended[..., :-2]
    conduct_next = conduct_extended[..., 2:]
    depth_prev = jnp.concatenate([solid[:, :1], solid[:, :-1]], 1)
    depth_next = jnp.concatenate([solid[:, 1:], solid[:, -1:]], 1)
    kdepth_prev = jnp.concatenate([conduct[:, :1], conduct[:, :-1]], 1)
    kdepth_next = jnp.concatenate([conduct[:, 1:], conduct[:, -1:]], 1)
    flow = (
        0.5 * (conduct + conduct_prev) * (stream_prev - solid)
        + 0.5 * (conduct + conduct_next) * (stream_next - solid)
        + 0.5 * (conduct + kdepth_prev) * (depth_prev - solid)
        + 0.5 * (conduct + kdepth_next) * (depth_next - solid)
    )
    updated = solid + SOLID_STEP * flow
    updated = updated.at[:, 0].add(SOLID_STEP * inflow)
    updated = updated.at[:, -1].add(SOLID_STEP * COOLING * (COOLANT - solid[:, -1]))
    return updated


def local(
    fluid_temp, stream_velocity, pitch_velocity, film_coeff, solid_temp, conductivity, face_owner
):
    span_cells, pitch_cells, stream_cells = fluid_temp.shape
    depth_cells = solid_temp.shape[1]
    block_count = lax.axis_size("blk")
    capacity = max(2, (pitch_cells + block_count - 1) // block_count)
    owners = face_owner.reshape(-1)
    onehot = (owners[:, None] == jnp.arange(block_count, dtype=jnp.int32)[None, :]).astype(
        jnp.float32
    )
    same_owner = owners[:, None] == owners[None, :]
    earlier = lax.broadcasted_iota(jnp.int32, (pitch_cells, pitch_cells), 0) < lax.broadcasted_iota(
        jnp.int32, (pitch_cells, pitch_cells), 1
    )
    slot_rank = jnp.sum((same_owner & earlier).astype(jnp.int32), axis=0)
    slot_table = (slot_rank[None, :] == jnp.arange(capacity, dtype=jnp.int32)[:, None]).astype(
        jnp.float32
    )
    placing = onehot.T[:, None, :] * slot_table[None, :, :]
    fluid = fluid_temp
    solid = solid_temp
    gas_rows = span_cells * pitch_cells
    for subiter in range(SUB):
        wall_row = solid[0, 0:1, :]
        wall_temp = jnp.dot(
            onehot,
            lax.all_gather(wall_row, "blk", axis=0, tiled=True),
            precision=lax.Precision.HIGHEST,
            preferred_element_type=jnp.float32,
        )
        flux = film_coeff * (fluid[0] - wall_temp)
        outgoing = jnp.einsum("ocb,bf->ocf", placing, flux, precision=lax.Precision.HIGHEST)
        received = lax.all_to_all(outgoing, "blk", split_axis=0, concat_axis=0, tiled=True)
        inflow = jnp.sum(received, axis=(0, 1))
        conduct = conductivity * (1.0 + 0.25 * jnp.tanh(solid))
        stacked = jnp.concatenate([fluid.reshape(gas_rows, stream_cells), solid[0], conduct[0]], 0)
        stream_ext = padded(stacked, (("blk", 1),), 1, False)
        pitch_extended = padded(fluid, (("sec", 1),), 1, True)
        fluid_stream = stream_ext[:gas_rows].reshape(span_cells, pitch_cells, stream_cells + 2)
        solid_stream = stream_ext[gas_rows : gas_rows + depth_cells][None]
        conduct_stream = stream_ext[gas_rows + depth_cells :][None]
        fluid = fluid_update(
            fluid, stream_velocity, pitch_velocity, flux, pitch_extended, fluid_stream
        )
        solid = solid_update(solid, conduct, inflow[None, :], solid_stream, conduct_stream)
    return (fluid, solid)


def solution(mesh):
    placed = (
        P(None, "sec", "blk"),
        P(None, "sec", "blk"),
        P(None, "sec", "blk"),
        P("sec", "blk"),
        P("sec", None, "blk"),
        P("sec", None, "blk"),
        P("sec", "blk", None, None),
    )
    return jax.shard_map(
        local,
        mesh=mesh,
        in_specs=placed,
        out_specs=(P(None, "sec", "blk"), P("sec", None, "blk")),
        check_vma=False,
    )
```

profile of v0, /device:TPU:64, one launch (start us, length us, event | category | flops | bytes accessed | tf_op | source)
XLA Modules:
  0.0 1452.0 jit_solution(16969111465341396685)
XLA Ops:
  0.6 0.8 fusion.151
  1.4 1.9 collective-permute-start
  3.3 5.4 collective-permute-start.1
  8.8 0.7 add_multiply_fusion.3
  9.5 1.0 pad_maximum_fusion.4
  10.5 0.1 fusion.142
  10.7 4.3 collective-permute-start.2
  15.0 7.6 collective-permute-start.3
  22.6 0.6 copy-done.8
  23.5 322.6 %all-gather = f32[96,1,128]{2,1,0:T(1,128)S(1)} all-gather(f32[1,1,128]{2,1,0:T(1,128)S(1)} %get-tuple-element.207), channel_id=2, replica_groups=mesh['sec'=8,'blk'=96] {'blk'}, dimensions={0}, use_global_device_ids=true | all-gather | bytes 49664 | tf_op jit(solution)/shard_map/all_gather | solution.py:101
  346.3 0.3 pad_maximum_fusion
  346.7 0.9 copy-done.1
  347.6 0.3 fusion.51
  347.9 0.5 copy-done.4
  348.4 0.2 constant_dynamic-update-slice_fusion.2
  348.6 0.4 fusion.66
  349.0 0.7 copy.13
  349.8 14.7 %all-to-all-start = ((f32[96,2,128]{2,1,0:T(2,128)}), f32[96,2,128]{2,1,0:T(2,128)S(1)}, u32[]{:S(2)}, u32[]{:S(2)}) async-start(f32[96,2,128]{2,1,0:T(2,128)} %copy.13), calls=%async_computation | async-start | bytes 196608 | tf_op jit(solution)/shard_map/all_to_all | solution.py:107
  364.5 1.9 collective-permute-start.4
  366.4 5.4 collective-permute-start.5
  371.9 9.4 all-to-all-done
  381.3 0.1 reduce_sum.46
  381.5 0.5 copy-done.6
  382.1 0.1 fusion.141
  382.3 2.1 collective-permute-start.6
  384.4 3.7 collective-permute-start.7
  388.1 317.8 %all-gather.1 = f32[96,1,128]{2,1,0:T(1,128)S(1)} all-gather(f32[1,1,128]{2,1,0:T(1,128)S(1)} %slice.737), channel_id=3, replica_groups=mesh['sec'=8,'blk'=96] {'blk'}, dimensions={0}, use_global_device_ids=true | all-gather | bytes 49664 | tf_op jit(solution)/shard_map/all_gather | solution.py:101
  705.9 0.3 pad_maximum_fusion.1
  706.3 0.3 fusion.37
  706.6 0.2 constant_dynamic-update-slice_fusion.1
  706.8 1.9 collective-permute-start.8
  708.7 5.4 collective-permute-start.9
  714.2 0.4 fusion.64
  714.6 0.7 copy.14
  715.3 8.5 all-to-all-start.1
  724.1 16.7 %all-to-all-done.1 = f32[96,2,128]{2,1,0:T(2,128)S(1)} async-done(((f32[96,2,128]{2,1,0:T(2,128)}), f32[96,2,128]{2,1,0:T(2,128)S(1)}, u32[]{:S(2)}, u32[]{:S(2)}) %all-to-all-start.1) | async-done | bytes 98336 | tf_op jit(solution)/shard_map/all_to_all | solution.py:107
  740.8 0.1 reduce_sum.47
  741.1 0.1 fusion.140
  741.2 2.1 collective-permute-start.10
  743.3 3.8 collective-permute-start.11
  747.1 317.8 %all-gather.2 = f32[96,1,128]{2,1,0:T(1,128)S(1)} all-gather(f32[1,1,128]{2,1,0:T(1,128)S(1)} %slice.761), channel_id=4, replica_groups=mesh['sec'=8,'blk'=96] {'blk'}, dimensions={0}, use_global_device_ids=true | all-gather | bytes 49664 | tf_op jit(solution)/shard_map/all_gather | solution.py:101
  1064.9 0.3 pad_maximum_fusion.2
  1065.2 0.3 fusion.23
  1065.5 0.2 constant_dynamic-update-slice_fusion
  1065.8 1.9 collective-permute-start.12
  1067.7 5.4 collective-permute-start.13
  1073.2 0.4 fusion.62
  1073.6 0.7 copy.15
  1074.3 8.3 all-to-all-start.2
  1082.9 16.7 %all-to-all-done.2 = f32[96,2,128]{2,1,0:T(2,128)S(1)} async-done(((f32[96,2,128]{2,1,0:T(2,128)}), f32[96,2,128]{2,1,0:T(2,128)S(1)}, u32[]{:S(2)}, u32[]{:S(2)}) %all-to-all-start.2) | async-done | bytes 98336 | tf_op jit(solution)/shard_map/all_to_all | solution.py:107
  1099.6 0.1 reduce_sum.48
  1099.9 0.1 fusion.139
  1100.1 2.1 collective-permute-start.14
  1102.1 4.0 collective-permute-start.15
  1106.1 317.8 %all-gather.3 = f32[96,1,128]{2,1,0:T(1,128)S(1)} all-gather(f32[1,1,128]{2,1,0:T(1,128)S(1)} %slice.785), channel_id=5, replica_groups=mesh['sec'=8,'blk'=96] {'blk'}, dimensions={0}, use_global_device_ids=true | all-gather | bytes 49664 | tf_op jit(solution)/shard_map/all_gather | solution.py:101
  1423.9 0.3 pad_maximum_fusion.3
  1424.2 0.3 fusion.9
  1424.5 0.2 fusion.68
  1424.8 0.4 fusion.60
  1425.2 0.7 copy.16
  1425.9 8.3 all-to-all-start.3
  1434.4 16.7 %all-to-all-done.3 = f32[96,2,128]{2,1,0:T(2,128)S(1)} async-done(((f32[96,2,128]{2,1,0:T(2,128)}), f32[96,2,128]{2,1,0:T(2,128)S(1)}, u32[]{:S(2)}, u32[]{:S(2)}) %all-to-all-start.3) | async-done | bytes 98336 | tf_op jit(solution)/shard_map/all_to_all | solution.py:107
  1451.2 0.1 reduce_sum.49
  1451.4 0.6 copy-done.7
  (92 shorter events, 1.9 us)
Async XLA Ops:
  0.6 8.2 copy-start.3
  1.4 345.2 %collective-permute-start = (f32[8,1,128]{2,1,0:T(1,128)S(1)}, f32[8,1,128]{2,1,0:T(1,128)S(1)}, u32[]{:S(2)}, u32[]{:S(2)}) collective-permute-start(f32[8,1,128]{2,1,0:T(1,128)S(1)} %get-tuple-element.184), channel_id=1, source_target_pairs={{0,96},{96,192},{192,288},{288,384},{384,480},{480,576},{576,672},... | collective-permute-start | bytes 12296 | tf_op jit(solution)/shard_map/ppermute | solution.py:24
  3.3 343.3 %collective-permute-start.1 = (f32[8,1,128]{2,1,0:T(1,128)S(1)}, f32[8,1,128]{2,1,0:T(1,128)S(1)}, u32[]{:S(2)}, u32[]{:S(2)}) collective-permute-start(f32[8,1,128]{2,1,0:T(1,128)S(1)} %get-tuple-element.185), channel_id=1, source_target_pairs={{96,0},{192,96},{288,192},{384,288},{480,384},{576,480},{672,576},... | collective-permute-start | bytes 12296 | tf_op jit(solution)/shard_map/ppermute | solution.py:27
  10.5 12.9 copy-start
  10.7 335.4 %collective-permute-start.2 = (f32[576,1]{1,0:T(8,128)S(1)}, f32[576,1]{1,0:T(8,128)S(1)}, u32[]{:S(2)}, u32[]{:S(2)}) collective-permute-start(f32[576,1]{1,0:T(8,128)S(1)} %get-tuple-element.166), channel_id=1, source_target_pairs={{0,1},{1,2},{2,3},{3,4},{4,5},{5,6},{6,7},{7,8},{8,9},{9,10},{10,1... | collective-permute-start | bytes 6920 | tf_op jit(solution)/shard_map/ppermute | solution.py:24
  15.0 331.2 %collective-permute-start.3 = (f32[576,1]{1,0:T(8,128)S(1)}, f32[576,1]{1,0:T(8,128)S(1)}, u32[]{:S(2)}, u32[]{:S(2)}) collective-permute-start(f32[576,1]{1,0:T(8,128)S(1)} %get-tuple-element.167), channel_id=1, source_target_pairs={{1,0},{2,1},{3,2},{4,3},{5,4},{6,5},{7,6},{8,7},{9,8},{10,9},{11,1... | collective-permute-start | bytes 6920 | tf_op jit(solution)/shard_map/ppermute | solution.py:27
  22.6 0.7 copy-start.8
  346.6 1.0 copy-start.1
  346.6 1.0 copy-start.2
  347.6 0.8 copy-start.4
  349.8 31.6 %all-to-all-start = ((f32[96,2,128]{2,1,0:T(2,128)}), f32[96,2,128]{2,1,0:T(2,128)S(1)}, u32[]{:S(2)}, u32[]{:S(2)}) async-start(f32[96,2,128]{2,1,0:T(2,128)} %copy.13), calls=%async_computation | async-start | bytes 196608 | tf_op jit(solution)/shard_map/all_to_all | solution.py:107
  364.5 341.8 %collective-permute-start.4 = (f32[8,1,128]{2,1,0:T(1,128)S(1)}, f32[8,1,128]{2,1,0:T(1,128)S(1)}, u32[]{:S(2)}, u32[]{:S(2)}) collective-permute-start(f32[8,1,128]{2,1,0:T(1,128)S(1)} %get-tuple-element.178), channel_id=1, source_target_pairs={{0,96},{96,192},{192,288},{288,384},{384,480},{480,576},{576,672},... | collective-permute-start | bytes 12296 | tf_op jit(solution)/shard_map/ppermute | solution.py:24
  366.4 339.8 %collective-permute-start.5 = (f32[8,1,128]{2,1,0:T(1,128)S(1)}, f32[8,1,128]{2,1,0:T(1,128)S(1)}, u32[]{:S(2)}, u32[]{:S(2)}) collective-permute-start(f32[8,1,128]{2,1,0:T(1,128)S(1)} %get-tuple-element.179), channel_id=1, source_target_pairs={{96,0},{192,96},{288,192},{384,288},{480,384},{576,480},{672,576},... | collective-permute-start | bytes 12296 | tf_op jit(solution)/shard_map/ppermute | solution.py:27
  381.3 0.7 copy-start.6
  382.3 323.6 %collective-permute-start.6 = (f32[576,1]{1,0:T(8,128)S(1)}, f32[576,1]{1,0:T(8,128)S(1)}, u32[]{:S(2)}, u32[]{:S(2)}) collective-permute-start(f32[576,1]{1,0:T(8,128)S(1)} %get-tuple-element.164), channel_id=1, source_target_pairs={{0,1},{1,2},{2,3},{3,4},{4,5},{5,6},{6,7},{7,8},{8,9},{9,10},{10,1... | collective-permute-start | bytes 6920 | tf_op jit(solution)/shard_map/ppermute | solution.py:24
  384.4 321.5 %collective-permute-start.7 = (f32[576,1]{1,0:T(8,128)S(1)}, f32[576,1]{1,0:T(8,128)S(1)}, u32[]{:S(2)}, u32[]{:S(2)}) collective-permute-start(f32[576,1]{1,0:T(8,128)S(1)} %get-tuple-element.165), channel_id=1, source_target_pairs={{1,0},{2,1},{3,2},{4,3},{5,4},{6,5},{7,6},{8,7},{9,8},{10,9},{11,1... | collective-permute-start | bytes 6920 | tf_op jit(solution)/shard_map/ppermute | solution.py:27
  706.8 358.4 %collective-permute-start.8 = (f32[8,1,128]{2,1,0:T(1,128)S(1)}, f32[8,1,128]{2,1,0:T(1,128)S(1)}, u32[]{:S(2)}, u32[]{:S(2)}) collective-permute-start(f32[8,1,128]{2,1,0:T(1,128)S(1)} %get-tuple-element.174), channel_id=1, source_target_pairs={{0,96},{96,192},{192,288},{288,384},{384,480},{480,576},{576,672},... | collective-permute-start | bytes 12296 | tf_op jit(solution)/shard_map/ppermute | solution.py:24
  708.7 356.5 %collective-permute-start.9 = (f32[8,1,128]{2,1,0:T(1,128)S(1)}, f32[8,1,128]{2,1,0:T(1,128)S(1)}, u32[]{:S(2)}, u32[]{:S(2)}) collective-permute-start(f32[8,1,128]{2,1,0:T(1,128)S(1)} %get-tuple-element.175), channel_id=1, source_target_pairs={{96,0},{192,96},{288,192},{384,288},{480,384},{576,480},{672,576},... | collective-permute-start | bytes 12296 | tf_op jit(solution)/shard_map/ppermute | solution.py:27
  715.3 25.5 %all-to-all-start.1 = ((f32[96,2,128]{2,1,0:T(2,128)}), f32[96,2,128]{2,1,0:T(2,128)S(1)}, u32[]{:S(2)}, u32[]{:S(2)}) async-start(f32[96,2,128]{2,1,0:T(2,128)} %copy.14), calls=%async_computation.1 | async-start | bytes 196608 | tf_op jit(solution)/shard_map/all_to_all | solution.py:107
  741.2 323.6 %collective-permute-start.10 = (f32[576,1]{1,0:T(8,128)S(1)}, f32[576,1]{1,0:T(8,128)S(1)}, u32[]{:S(2)}, u32[]{:S(2)}) collective-permute-start(f32[576,1]{1,0:T(8,128)S(1)} %get-tuple-element.162), channel_id=1, source_target_pairs={{0,1},{1,2},{2,3},{3,4},{4,5},{5,6},{6,7},{7,8},{8,9},{9,10},{10,1... | collective-permute-start | bytes 6920 | tf_op jit(solution)/shard_map/ppermute | solution.py:24
  743.3 321.6 %collective-permute-start.11 = (f32[576,1]{1,0:T(8,128)S(1)}, f32[576,1]{1,0:T(8,128)S(1)}, u32[]{:S(2)}, u32[]{:S(2)}) collective-permute-start(f32[576,1]{1,0:T(8,128)S(1)} %get-tuple-element.163), channel_id=1, source_target_pairs={{1,0},{2,1},{3,2},{4,3},{5,4},{6,5},{7,6},{8,7},{9,8},{10,9},{11,1... | collective-permute-start | bytes 6920 | tf_op jit(solution)/shard_map/ppermute | solution.py:27
  1065.8 358.4 %collective-permute-start.12 = (f32[8,1,128]{2,1,0:T(1,128)S(1)}, f32[8,1,128]{2,1,0:T(1,128)S(1)}, u32[]{:S(2)}, u32[]{:S(2)}) collective-permute-start(f32[8,1,128]{2,1,0:T(1,128)S(1)} %get-tuple-element.170), channel_id=1, source_target_pairs={{0,96},{96,192},{192,288},{288,384},{384,480},{480,576},{576,672},... | collective-permute-start | bytes 12296 | tf_op jit(solution)/shard_map/ppermute | solution.py:24
  1067.7 356.5 %collective-permute-start.13 = (f32[8,1,128]{2,1,0:T(1,128)S(1)}, f32[8,1,128]{2,1,0:T(1,128)S(1)}, u32[]{:S(2)}, u32[]{:S(2)}) collective-permute-start(f32[8,1,128]{2,1,0:T(1,128)S(1)} %get-tuple-element.171), channel_id=1, source_target_pairs={{96,0},{192,96},{288,192},{384,288},{480,384},{576,480},{672,576},... | collective-permute-start | bytes 12296 | tf_op jit(solution)/shard_map/ppermute | solution.py:27
  1074.3 25.3 %all-to-all-start.2 = ((f32[96,2,128]{2,1,0:T(2,128)}), f32[96,2,128]{2,1,0:T(2,128)S(1)}, u32[]{:S(2)}, u32[]{:S(2)}) async-start(f32[96,2,128]{2,1,0:T(2,128)} %copy.15), calls=%async_computation.2 | async-start | bytes 196608 | tf_op jit(solution)/shard_map/all_to_all | solution.py:107
  1100.1 323.8 %collective-permute-start.14 = (f32[576,1]{1,0:T(8,128)S(1)}, f32[576,1]{1,0:T(8,128)S(1)}, u32[]{:S(2)}, u32[]{:S(2)}) collective-permute-start(f32[576,1]{1,0:T(8,128)S(1)} %get-tuple-element.160), channel_id=1, source_target_pairs={{0,1},{1,2},{2,3},{3,4},{4,5},{5,6},{6,7},{7,8},{8,9},{9,10},{10,1... | collective-permute-start | bytes 6920 | tf_op jit(solution)/shard_map/ppermute | solution.py:24
  1102.1 321.8 %collective-permute-start.15 = (f32[576,1]{1,0:T(8,128)S(1)}, f32[576,1]{1,0:T(8,128)S(1)}, u32[]{:S(2)}, u32[]{:S(2)}) collective-permute-start(f32[576,1]{1,0:T(8,128)S(1)} %get-tuple-element.161), channel_id=1, source_target_pairs={{1,0},{2,1},{3,2},{4,3},{5,4},{6,5},{7,6},{8,7},{9,8},{10,9},{11,1... | collective-permute-start | bytes 6920 | tf_op jit(solution)/shard_map/ppermute | solution.py:27
  1424.8 1.1 copy-start.5
  1425.9 25.3 %all-to-all-start.3 = ((f32[96,2,128]{2,1,0:T(2,128)}), f32[96,2,128]{2,1,0:T(2,128)S(1)}, u32[]{:S(2)}, u32[]{:S(2)}) async-start(f32[96,2,128]{2,1,0:T(2,128)} %copy.16), calls=%async_computation.3 | async-start | bytes 196608 | tf_op jit(solution)/shard_map/all_to_all | solution.py:107
  1451.4 0.6 copy-start.7
where the time goes:
time: 1450 us
  blocking collectives  1280 us (88%)
  starting transfers between devices  98.9 us (7%)
  waiting for transfers between devices  59.6 us (4%)
    all_gather x4, blocking collectives, local(): lax.all_gather(wall_row, 'blk', axis=0, tiled=True)  1280 us
    all_to_all x4, waiting for transfers between devices, local(): lax.all_to_all(outgoing, 'blk', split_axis=0, concat_axis=0, tiled=True)  59.6 us
    ppermute x8, starting transfers between devices, padded(): lax.ppermute(lax.slice_in_dim(block, 0, width, axis=dim), axis, backward)  40.8 us
    all_to_all x4, starting transfers between devices, local(): lax.all_to_all(outgoing, 'blk', split_axis=0, concat_axis=0, tiled=True)  39.9 us
  transfers between devices with their start and end apart: 20, of which 4 were waited for; matrix products, arithmetic and copies ran while one was open for 1% of the time, Pallas kernels for 0%

commit v1 on v0

v1 whole, which is shorter than its diff:
```python
import jax
import jax.numpy as jnp
from jax import lax
from jax.experimental import pallas as pl
from jax.experimental.pallas import tpu as pltpu
from jax.sharding import PartitionSpec as P

SUB = 4
F32 = jnp.float32
MESH = pl.DeviceIdType.MESH

ADVECT = 0.4
SPREAD = 0.04
WALL = 0.4
SOLID_STEP = 0.04
COOLING = 0.5
COOLANT = -1.0

FZ, FP, FS, SD = 8, 64, 128, 32
N_SEC, N_BLK = 8, 96
NX, NY, NZ = 4, 2, 12
TILES = FP // 8
PLANE = [(2, 1), (1, 1), (3, 1), (0, 1), (2, 0), (1, 0), (3, 0), (0, 0)]
HIGHEST = lax.Precision.HIGHEST


def slot_of(dx, dy, dz):
    return (dx * NY + dy) * NZ + dz


def roll(value, shift, axis):
    return pltpu.roll(value, shift, axis)


def kernel(
    fluid_in, stream_in, pitch_in, film_in, solid_in, cond_in, owner_ref,
    fluid_out, solid_out,
    field, vel, coef, film, solid, cond, pick, place, base0, packed,
    g_send, g_recv, table, pitch_send, pitch_recv, edge_send, edge_recv, rim_send, rim_recv,
    io_sem, g_ssem, g_rsem, t_ssem, t_rsem, h_ssem, h_rsem, r_ssem, r_rsem,
):
    sec = lax.axis_index("sec")
    blk = lax.axis_index("blk")
    x, y, z = blk // (NY * NZ), lax.rem(blk // NZ, NY), lax.rem(blk, NZ)
    sec_ids = [lax.rem(sec + N_SEC - 1, N_SEC), lax.rem(sec + 1, N_SEC)]
    blk_ids = [lax.rem(blk + N_BLK - 1, N_BLK), lax.rem(blk + 1, N_BLK)]
    plane = {
        (dx, dy): lax.rem(x + dx, NX) * (NY * NZ) + lax.rem(y + dy, NY) * NZ for dx, dy in PLANE
    }

    def each_peer(act):
        def step(t, carry):
            half = (t + 1) // 2
            dz = 6 + half * (1 - 2 * lax.rem(t, 2))
            far = lax.rem(z + dz, NZ)
            for dx, dy in PLANE:
                act(plane[dx, dy] + far, slot_of(dx, dy, dz), slot_of((NX - dx) % NX, dy, NZ - dz))
            return carry

        lax.fori_loop(0, NZ - 1, step, 0)
        for dx, dy in PLANE[:-1]:
            act(plane[dx, dy] + z, slot_of(dx, dy, 0), slot_of((NX - dx) % NX, dy, 0))

    loads = [
        pltpu.make_async_copy(fluid_in, field.at[0, :, pl.ds(8, FP), :], io_sem.at[0]),
        pltpu.make_async_copy(film_in, film, io_sem.at[1]),
        pltpu.make_async_copy(solid_in.at[0], solid, io_sem.at[2]),
        pltpu.make_async_copy(cond_in.at[0], cond, io_sem.at[3]),
        pltpu.make_async_copy(stream_in, vel.at[0], io_sem.at[4]),
        pltpu.make_async_copy(pitch_in, vel.at[1], io_sem.at[5]),
    ]
    for copy in loads:
        copy.start()

    barrier = pltpu.get_barrier_semaphore()
    each_peer(
        lambda peer, there, here: pl.semaphore_signal(
            barrier, inc=1, device_id={"blk": peer}, device_id_type=MESH
        )
    )
    for target in sec_ids:
        pl.semaphore_signal(barrier, inc=1, device_id={"sec": target}, device_id_type=MESH)

    owner = owner_ref[0, 0]
    slot = slot_of(
        lax.rem(owner // (NY * NZ) - x + NX, NX),
        lax.rem(lax.rem(owner // NZ, NY) - y + NY, NY),
        lax.rem(lax.rem(owner, NZ) - z + NZ, NZ),
    )
    wide = jnp.broadcast_to(slot, (FP, 128))
    chosen = (wide == lax.broadcasted_iota(jnp.int32, (FP, 128), 1)).astype(F32)
    pick[...] = chosen[:, :N_BLK]
    place[...] = chosen.T[:N_BLK]

    lane = lax.broadcasted_iota(jnp.int32, (8, 128), 1)
    pair = lane // 2
    even = lax.rem(lane, 2) == 0
    wide_lane = lax.broadcasted_iota(jnp.int32, (FP, 128), 1)
    keep_low = (blk != 0).astype(F32)
    keep_high = (blk != N_BLK - 1).astype(F32)

    def gathered(k):
        return jnp.dot(
            pick[...], table.at[k].reshape(N_BLK, FS)[...], precision=HIGHEST,
            preferred_element_type=F32,
        )

    def placed(value):
        return jnp.dot(place[...], value, precision=HIGHEST, preferred_element_type=F32)

    def both_ends(tile, index):
        return jnp.where(pair == index, roll(tile, lax.rem(2 * index + 1, 128), 1), 0.0)

    def layer_ends(layer, q):
        total = both_ends(layer[0:8], q * TILES)
        for t in range(1, TILES):
            total = total + both_ends(layer[8 * t : 8 * t + 8], q * TILES + t)
        return total

    def joined(below, above):
        return jnp.where(even, roll(above, 127, 1) * keep_high, roll(below, 1, 1) * keep_low)

    def shifted(tile, ends, index):
        rim = roll(ends, lax.rem(255 - 2 * index, 128), 1)
        low = jnp.where(lane == 0, rim, roll(tile, 1, 1))
        high = jnp.where(lane == 127, rim, roll(tile, 127, 1))
        return low, high

    def send_halo(k):
        for i in range(2):
            pltpu.make_async_remote_copy(
                pitch_send.at[k, i], pitch_recv.at[k, 1 - i], h_ssem.at[k, i], h_rsem.at[k, 1 - i],
                device_id={"sec": sec_ids[i]}, device_id_type=MESH,
            ).start()
            pltpu.make_async_remote_copy(
                edge_send.at[k], edge_recv.at[k, 1 - i], h_ssem.at[k, 2 + i],
                h_rsem.at[k, 3 - i], device_id={"blk": blk_ids[i]}, device_id_type=MESH,
            ).start()

    def take_halo(k):
        for i in range(2):
            here = pitch_recv.at[k, i]
            pltpu.make_async_copy(here, here, h_rsem.at[k, i]).wait()
            here = edge_recv.at[k, i]
            pltpu.make_async_copy(here, here, h_rsem.at[k, 2 + i]).wait()
        for q in range(FZ):
            field[k % 2, q, 7:8, :] = pitch_recv[k, 0, q : q + 1, :]
            field[k % 2, q, FP + 8 : FP + 9, :] = pitch_recv[k, 1, q : q + 1, :]
        return joined(edge_recv[k, 0], edge_recv[k, 1])

    def send_rim(k):
        for i in range(2):
            pltpu.make_async_remote_copy(
                rim_send.at[k], rim_recv.at[k, 1 - i], r_ssem.at[k, i], r_rsem.at[k, 1 - i],
                device_id={"blk": blk_ids[i]}, device_id_type=MESH,
            ).start()

    def take_rim(k):
        for i in range(2):
            here = rim_recv.at[k, i]
            pltpu.make_async_copy(here, here, r_rsem.at[k, i]).wait()
        return joined(rim_recv[k, 0], rim_recv[k, 1])

    def send_flux(first, count, sem):
        def act(peer, there, here):
            for c in range(first, first + count):
                pltpu.make_async_remote_copy(
                    g_send.at[c, there], g_recv.at[c, here], g_ssem.at[sem], g_rsem.at[sem],
                    device_id={"blk": peer}, device_id_type=MESH,
                ).start()

        each_peer(act)

    def take_flux(first, count, sem):
        here = g_recv.at[pl.ds(first, count), pl.ds(1, N_BLK - 1)]
        pltpu.make_async_copy(here, here, g_rsem.at[sem]).wait()
        out = []
        for c in range(first, first + count):
            g_recv[c, 0] = g_send[c, 0]
            out.append(
                jnp.sum(g_recv.at[c].reshape(N_BLK, FS)[...], axis=0, keepdims=True)
            )
        return out

    def send_wall(k):
        def act(peer, there, here):
            pltpu.make_async_remote_copy(
                table.at[k, 0], table.at[k, here], t_ssem.at[k], t_rsem.at[k],
                device_id={"blk": peer}, device_id_type=MESH,
            ).start()

        each_peer(act)

    def take_wall(k):
        here = table.at[k, pl.ds(1, N_BLK - 1)]
        pltpu.make_async_copy(here, here, t_rsem.at[k]).wait()

    def stencil(k, q, ends):
        cur = k % 2
        centre = field[cur, q, pl.ds(8, FP), :]
        before = field[cur, q, pl.ds(7, FP), :]
        after = field[cur, q, pl.ds(9, FP), :]
        below = field[cur, jnp.maximum(q - 1, 0), pl.ds(8, FP), :]
        above = field[cur, jnp.minimum(q + 1, FZ - 1), pl.ds(8, FP), :]
        lows, highs = [], []
        for t in range(TILES):
            low, high = shifted(centre[8 * t : 8 * t + 8], ends, q * TILES + t)
            lows.append(low)
            highs.append(high)
        low, high = jnp.concatenate(lows, 0), jnp.concatenate(highs, 0)
        return (
            coef[0, q] * centre
            + coef[1, q] * before
            + coef[2, q] * after
            + coef[3, q] * low
            + SPREAD * (high + below + above)
        )

    def store_layer(k, q, layer):
        field[k % 2, q, pl.ds(8, FP), :] = layer
        if k < SUB:
            pitch_send[k, 0, pl.ds(q, 1), :] = layer[0:1]
            pitch_send[k, 1, pl.ds(q, 1), :] = layer[FP - 1 : FP]

    def wall_layer(k, ends):
        layer = stencil(k, 0, ends) - WALL * film[...] * field[k % 2, 0, pl.ds(8, FP), :]
        base0[...] = layer
        return layer

    def other_layers(k, ends):
        def step(q, total):
            layer = stencil(k, q, ends)
            store_layer(k + 1, q, layer)
            if k + 1 < SUB:
                total = total + layer_ends(layer, q)
            return total

        packed[...] = lax.fori_loop(1, FZ, step, jnp.zeros((8, 128), F32))

    def finish_layer(k):
        take_wall(k)
        layer = base0[...] + WALL * film[...] * gathered(k)
        store_layer(k + 1, 0, layer)
        if k + 1 < SUB:
            edge_send[k + 1] = packed[...] + layer_ends(layer, 0)
            send_halo(k + 1)

    def conduct_of(metal):
        return cond[...] * (1.0 + 0.25 * jnp.tanh(metal))

    def pack_rim(k, metal, conduct):
        total = jnp.zeros((8, 128), F32)
        for t in range(SD // 8):
            total = total + both_ends(metal[8 * t : 8 * t + 8], t)
            total = total + both_ends(conduct[8 * t : 8 * t + 8], SD // 8 + t)
        rim_send[k] = total

    row = lax.broadcasted_iota(jnp.int32, (SD, FS), 0)

    def metal_step(metal, conduct, ends):
        def neighbours(value, offset):
            lows, highs = [], []
            for t in range(SD // 8):
                low, high = shifted(value[8 * t : 8 * t + 8], ends, offset + t)
                lows.append(low)
                highs.append(high)
            up = jnp.where(row == 0, value, roll(value, 1, 0))
            down = jnp.where(row == SD - 1, value, roll(value, SD - 1, 0))
            return jnp.concatenate(lows, 0), jnp.concatenate(highs, 0), up, down

        flow = jnp.zeros((SD, FS), F32)
        for near, k_near in zip(neighbours(metal, 0), neighbours(conduct, SD // 8)):
            flow = flow + 0.5 * (conduct + k_near) * (near - metal)
        cooling = jnp.where(row == SD - 1, COOLING * (COOLANT - metal), 0.0)
        return metal + SOLID_STEP * (flow + cooling)

    def heated(metal, inflow):
        return metal + jnp.where(row == 0, SOLID_STEP * inflow, 0.0)

    def publish(k, metal):
        table[k, 0] = metal[0:1]
        conduct = conduct_of(metal)
        pack_rim(k, metal, conduct)
        return conduct

    for copy in loads[:4]:
        copy.wait()
    h = film[...]
    v = h * field[0, 0, pl.ds(8, FP), :]
    firsts = placed(jnp.concatenate([v, h, WALL * h * h], 1))
    for c, dest in enumerate((0, 1, 3)):
        g_send.at[dest].reshape(N_BLK, FS)[...] = firsts[:, FS * c : FS * c + FS]
    metal = solid[...]
    conduct = publish(0, metal)

    def first_ends(q, total):
        layer = field[0, q, pl.ds(8, FP), :]
        pitch_send[0, 0, pl.ds(q, 1), :] = layer[0:1]
        pitch_send[0, 1, pl.ds(q, 1), :] = layer[FP - 1 : FP]
        return total + layer_ends(layer, q)

    edge_send[0] = lax.fori_loop(0, FZ, first_ends, jnp.zeros((8, 128), F32))
    for copy in loads[4:]:
        copy.wait()

    def coefficients(q, carry):
        u, w = vel[0, q], vel[1, q]
        coef[0, q] = (1.0 - 6.0 * SPREAD) - ADVECT * (u + jnp.abs(w))
        coef[1, q] = SPREAD + ADVECT * jnp.maximum(w, 0.0)
        coef[2, q] = SPREAD + ADVECT * jnp.maximum(-w, 0.0)
        coef[3, q] = SPREAD + ADVECT * u
        return carry

    lax.fori_loop(0, FZ, coefficients, 0)
    pl.semaphore_wait(barrier, N_BLK - 1 + 2)

    def flux_ahead(dest, layer):
        g_send.at[dest].reshape(N_BLK, FS)[...] = placed(film[...] * layer)

    send_halo(0)
    send_wall(0)
    send_flux(0, 2, 0)
    send_rim(0)
    ends = take_halo(0)
    flux_ahead(2, wall_layer(0, ends))
    send_flux(2, 2, 1)
    other_layers(0, ends)
    calm = metal_step(metal, conduct, take_rim(0))
    finish_layer(0)
    g0, total_h = take_flux(0, 2, 0)
    wall0 = metal[0:1]
    metal = heated(calm, g0 - wall0 * total_h)
    conduct = publish(1, metal)
    send_wall(1)
    send_rim(1)
    ends = take_halo(1)
    flux_ahead(4, wall_layer(1, ends))
    send_flux(4, 1, 2)
    other_layers(1, ends)
    calm = metal_step(metal, conduct, take_rim(1))
    wall1 = metal[0:1]
    g1, total_f = take_flux(2, 2, 1)
    metal = heated(calm, g1 + wall0 * total_f - wall1 * total_h)
    conduct = publish(2, metal)
    send_wall(2)
    send_rim(2)
    finish_layer(1)
    calm = metal_step(metal, conduct, take_rim(2))
    wall2 = metal[0:1]
    ends = take_halo(2)
    flux_ahead(5, wall_layer(2, ends))
    send_flux(5, 1, 3)
    (g2,) = take_flux(4, 1, 2)
    metal = heated(calm, g2 + wall1 * total_f - wall2 * total_h)
    conduct = publish(3, metal)
    send_wall(3)
    send_rim(3)
    other_layers(2, ends)
    finish_layer(2)
    wall3 = metal[0:1]
    ends = take_halo(3)
    wall_layer(3, ends)
    other_layers(3, ends)
    rest = pltpu.make_async_copy(
        field.at[0, pl.ds(1, FZ - 1), pl.ds(8, FP), :], fluid_out.at[pl.ds(1, FZ - 1)], io_sem.at[0]
    )
    rest.start()
    calm = metal_step(metal, conduct, take_rim(3))
    finish_layer(3)
    last = pltpu.make_async_copy(
        field.at[0, 0, pl.ds(8, FP), :], fluid_out.at[0], io_sem.at[1]
    )
    last.start()
    (g3,) = take_flux(5, 1, 3)
    solid[...] = heated(calm, g3 + wall2 * total_f - wall3 * total_h)
    metal_copy = pltpu.make_async_copy(solid, solid_out.at[0], io_sem.at[2])
    metal_copy.start()

    for first, count, sem in ((0, 2, 0), (2, 2, 1), (4, 1, 2), (5, 1, 3)):
        sent = g_send.at[pl.ds(first, count), pl.ds(1, N_BLK - 1)]
        pltpu.make_async_copy(sent, sent, g_ssem.at[sem]).wait()
    for k in range(SUB):
        sent = table.at[k, pl.ds(1, N_BLK - 1)]
        pltpu.make_async_copy(sent, sent, t_ssem.at[k]).wait()
        for i in range(2):
            sent = pitch_send.at[k, i]
            pltpu.make_async_copy(sent, sent, h_ssem.at[k, i]).wait()
            sent = edge_send.at[k]
            pltpu.make_async_copy(sent, sent, h_ssem.at[k, 2 + i]).wait()
            sent = rim_send.at[k]
            pltpu.make_async_copy(sent, sent, r_ssem.at[k, i]).wait()
    rest.wait()
    last.wait()
    metal_copy.wait()


def local(
    fluid_temp, stream_velocity, pitch_velocity, film_coeff, solid_temp, conductivity, face_owner
):
    dma = pltpu.SemaphoreType.DMA
    anywhere = pl.BlockSpec(memory_space=pl.ANY)
    return pl.pallas_call(
        kernel,
        out_shape=(
            jax.ShapeDtypeStruct((FZ, FP, FS), F32),
            jax.ShapeDtypeStruct((1, SD, FS), F32),
        ),
        in_specs=[anywhere] * 6 + [pl.BlockSpec(memory_space=pltpu.VMEM)],
        out_specs=(anywhere, anywhere),
        scratch_shapes=[
            pltpu.VMEM((2, FZ, FP + 16, FS), F32),
            pltpu.VMEM((2, FZ, FP, FS), F32),
            pltpu.VMEM((4, FZ, FP, FS), F32),
            pltpu.VMEM((FP, FS), F32),
            pltpu.VMEM((SD, FS), F32),
            pltpu.VMEM((SD, FS), F32),
            pltpu.VMEM((FP, N_BLK), F32),
            pltpu.VMEM((N_BLK, FP), F32),
            pltpu.VMEM((FP, FS), F32),
            pltpu.VMEM((8, FS), F32),
            pltpu.VMEM((6, N_BLK, 1, FS), F32),
            pltpu.VMEM((6, N_BLK, 1, FS), F32),
            pltpu.VMEM((SUB, N_BLK, 1, FS), F32),
            pltpu.VMEM((SUB, 2, FZ, FS), F32),
            pltpu.VMEM((SUB, 2, FZ, FS), F32),
            pltpu.VMEM((SUB, 8, FS), F32),
            pltpu.VMEM((SUB, 2, 8, FS), F32),
            pltpu.VMEM((SUB, 8, FS), F32),
            pltpu.VMEM((SUB, 2, 8, FS), F32),
            dma((6,)), dma((4,)), dma((4,)), dma((SUB,)), dma((SUB,)),
            dma((SUB, 4)), dma((SUB, 4)), dma((SUB, 2)), dma((SUB, 2)),
        ],
        compiler_params=pltpu.CompilerParams(collective_id=0, has_side_effects=True),
    )(fluid_temp, stream_velocity, pitch_velocity, film_coeff, solid_temp, conductivity, face_owner)


def solution(mesh):
    placed = (
        P(None, "sec", "blk"),
        P(None, "sec", "blk"),
        P(None, "sec", "blk"),
        P("sec", "blk"),
        P("sec", None, "blk"),
        P("sec", None, "blk"),
        P("sec", "blk", None, None),
    )
    return jax.shard_map(
        local,
        mesh=mesh,
        in_specs=placed,
        out_specs=(P(None, "sec", "blk"), P("sec", None, "blk")),
        check_vma=False,
    )
```

time: 1450 us -> 69.2 us (0.05)
  the two profiles are of different devices: /device:TPU:64 before, /device:TPU:8 now
where the time goes in v1:
time: 69.2 us; the launch traced here: 69 us
  Pallas kernels  64.7 us (93%)
  local copies, waits for them, and re-layouts  3.64 us (5%)
    pallas_call x1, Pallas kernels, local(): pl.pallas_call(kernel, out_shape=(jax.ShapeDtypeStruct((FZ, FP, FS), F32)...  64.7 us
    unnamed x5, local copies, waits for them, and re-layouts  3.64 us

profile of v1, /device:TPU:8, one launch (start us, length us, event | category | flops | bytes accessed | tf_op | source)
XLA Modules:
  0.0 69.0 jit_solution(9503904761126767415)
XLA Ops:
  0.6 1.4 %copy.9.owner_ref = s32[1,1,64,1]{3,2,1,0:T(8,128)} copy(s32[1,1,64,1]{2,3,1,0:T(1,128)} %param.13) | data formatting | bytes 512 | tf_op args[6]
  2.0 64.7 %shard_map.86 = (f32[8,64,128]{2,1,0:T(8,128)}, f32[1,32,128]{2,1,0:T(8,128)}) custom-call(f32[8,64,128]{2,1,0:T(8,128)} %fluid_in.1, f32[8,64,128]{2,1,0:T(8,128)} %stream_in.1, f32[8,64,128]{2,1,0:T(8,128)} %pitch_in.1, f32[64,128]{1,0:T(8,128)} %film_in.1, f32[1,32,128]{2,1,0:T(8,128)} %solid_in.1, f32[1,32,128]{2,1,0:T(8,128)} %cond_in.1, ...), custom_call_target="tpu_custom_call" | custom-call | tf_op jit(solution)/shard_map/pallas_call | solution.py:402
  66.7 0.0 copy-start
  66.7 1.7 %copy.12 = f32[8,64,128]{2,1,0:T(8,128)} copy(f32[8,64,128]{2,1,0:T(8,128)} %get-tuple-element.4) | data formatting | bytes 524288
  68.4 0.0 copy-done
  68.4 0.6 copy.13
Async XLA Ops:
  66.7 1.7 %copy-start = (f32[1,32,128]{2,1,0:T(8,128)S(1)}, f32[1,32,128]{2,1,0:T(8,128)}, u32[]{:S(2)}) copy-start(f32[1,32,128]{2,1,0:T(8,128)} %get-tuple-element.5) | copy-start | bytes 49156

commit v2 on v1

--- a/solution.py
+++ b/solution.py
@@ -7,6 +7,7 @@
 
 SUB = 4
 F32 = jnp.float32
+BF16 = jnp.bfloat16
 MESH = pl.DeviceIdType.MESH
 
 ADVECT = 0.4
@@ -21,7 +22,6 @@
 NX, NY, NZ = 4, 2, 12
 TILES = FP // 8
 PLANE = [(2, 1), (1, 1), (3, 1), (0, 1), (2, 0), (1, 0), (3, 0), (0, 0)]
-HIGHEST = lax.Precision.HIGHEST
 
 
 def slot_of(dx, dy, dz):
@@ -33,11 +33,12 @@
 
 
 def kernel(
-    fluid_in, stream_in, pitch_in, film_in, solid_in, cond_in, owner_ref,
+    fluid_in, stream_in, pitch_in, film_in, solid_in, cond_in, owner_in,
     fluid_out, solid_out,
-    field, vel, coef, film, solid, cond, pick, place, base0, packed,
+    field, vel, coef, film, solid, cond, owners, pick, place, base0,
+    const_send, const_recv, edge_film, edge_fix,
     g_send, g_recv, table, pitch_send, pitch_recv, edge_send, edge_recv, rim_send, rim_recv,
-    io_sem, g_ssem, g_rsem, t_ssem, t_rsem, h_ssem, h_rsem, r_ssem, r_rsem,
+    io_sem, g_ssem, g_rsem, t_ssem, t_rsem, h_ssem, h_rsem, r_ssem, r_rsem, c_ssem, c_rsem,
 ):
     sec = lax.axis_index("sec")
     blk = lax.axis_index("blk")
@@ -62,6 +63,7 @@
             act(plane[dx, dy] + z, slot_of(dx, dy, 0), slot_of((NX - dx) % NX, dy, 0))
 
     loads = [
+        pltpu.make_async_copy(owner_in, owners, io_sem.at[6]),
         pltpu.make_async_copy(fluid_in, field.at[0, :, pl.ds(8, FP), :], io_sem.at[0]),
         pltpu.make_async_copy(film_in, film, io_sem.at[1]),
         pltpu.make_async_copy(solid_in.at[0], solid, io_sem.at[2]),
@@ -81,16 +83,21 @@
     for target in sec_ids:
         pl.semaphore_signal(barrier, inc=1, device_id={"sec": target}, device_id_type=MESH)
 
-    owner = owner_ref[0, 0]
-    slot = slot_of(
-        lax.rem(owner // (NY * NZ) - x + NX, NX),
-        lax.rem(lax.rem(owner // NZ, NY) - y + NY, NY),
-        lax.rem(lax.rem(owner, NZ) - z + NZ, NZ),
-    )
-    wide = jnp.broadcast_to(slot, (FP, 128))
-    chosen = (wide == lax.broadcasted_iota(jnp.int32, (FP, 128), 1)).astype(F32)
-    pick[...] = chosen[:, :N_BLK]
-    place[...] = chosen.T[:N_BLK]
+    loads[0].wait()
+    owner = owners[...]
+
+    def one_hot(owner):
+        slot = slot_of(
+            lax.rem(owner // (NY * NZ) - x + NX, NX),
+            lax.rem(lax.rem(owner // NZ, NY) - y + NY, NY),
+            lax.rem(lax.rem(owner, NZ) - z + NZ, NZ),
+        )
+        wide = jnp.broadcast_to(slot, (128, FP))
+        return (wide == lax.broadcasted_iota(jnp.int32, (128, FP), 0)).astype(F32)
+
+    chosen = one_hot(owner)
+    place[...] = chosen[:N_BLK].astype(BF16)
+    pick[0:FP] = chosen.T[:, :N_BLK].astype(BF16)
 
     lane = lax.broadcasted_iota(jnp.int32, (8, 128), 1)
     pair = lane // 2
@@ -99,14 +106,19 @@
     keep_low = (blk != 0).astype(F32)
     keep_high = (blk != N_BLK - 1).astype(F32)
 
-    def gathered(k):
-        return jnp.dot(
-            pick[...], table.at[k].reshape(N_BLK, FS)[...], precision=HIGHEST,
-            preferred_element_type=F32,
-        )
+    def selected(ones, value):
+        high = value.astype(BF16)
+        rest = value - high.astype(F32)
+        middle = rest.astype(BF16)
+        low = (rest - middle.astype(F32)).astype(BF16)
+        dot = lambda part: jnp.dot(ones, part, preferred_element_type=F32)
+        return (dot(low) + dot(middle)) + dot(high)
+
+    def gathered(k, rows):
+        return selected(pick[0:rows], table.at[k].reshape(N_BLK, FS)[...])
 
     def placed(value):
-        return jnp.dot(place[...], value, precision=HIGHEST, preferred_element_type=F32)
+        return selected(place[...], value)
 
     def both_ends(tile, index):
         return jnp.where(pair == index, roll(tile, lax.rem(2 * index + 1, 128), 1), 0.0)
@@ -126,12 +138,30 @@
         high = jnp.where(lane == 127, rim, roll(tile, 127, 1))
         return low, high
 
-    def send_halo(k):
+    def send_pitch(k):
         for i in range(2):
             pltpu.make_async_remote_copy(
                 pitch_send.at[k, i], pitch_recv.at[k, 1 - i], h_ssem.at[k, i], h_rsem.at[k, 1 - i],
                 device_id={"sec": sec_ids[i]}, device_id_type=MESH,
             ).start()
+
+    def send_const():
+        for i in range(2):
+            pltpu.make_async_remote_copy(
+                const_send, const_recv.at[1 - i], c_ssem.at[i], c_rsem.at[1 - i],
+                device_id={"blk": blk_ids[i]}, device_id_type=MESH,
+            ).start()
+
+    def take_const():
+        for i in range(2):
+            here = const_recv.at[i]
+            pltpu.make_async_copy(here, here, c_rsem.at[i]).wait()
+            beside = one_hot(const_recv[i, 1, 0:1, 0:FP].astype(jnp.int32))
+            pick[FP * (i + 1) : FP * (i + 2)] = beside.T[:, :N_BLK].astype(BF16)
+        edge_film[...] = joined(const_recv[0, 0], const_recv[1, 0])
+
+    def send_edge(k):
+        for i in range(2):
             pltpu.make_async_remote_copy(
                 edge_send.at[k], edge_recv.at[k, 1 - i], h_ssem.at[k, 2 + i],
                 h_rsem.at[k, 3 - i], device_id={"blk": blk_ids[i]}, device_id_type=MESH,
@@ -146,7 +176,8 @@
         for q in range(FZ):
             field[k % 2, q, 7:8, :] = pitch_recv[k, 0, q : q + 1, :]
             field[k % 2, q, FP + 8 : FP + 9, :] = pitch_recv[k, 1, q : q + 1, :]
-        return joined(edge_recv[k, 0], edge_recv[k, 1])
+        ends = joined(edge_recv[k, 0], edge_recv[k, 1])
+        return ends + edge_fix[...] if k else ends
 
     def send_rim(k):
         for i in range(2):
@@ -181,6 +212,20 @@
                 jnp.sum(g_recv.at[c].reshape(N_BLK, FS)[...], axis=0, keepdims=True)
             )
         return out
+
+    def send_first():
+        def act(peer, there, here):
+            pltpu.make_async_remote_copy(
+                table.at[0, 0], table.at[0, here], t_ssem.at[0], t_rsem.at[0],
+                device_id={"blk": peer}, device_id_type=MESH,
+            ).start()
+            for c in range(2):
+                pltpu.make_async_remote_copy(
+                    g_send.at[c, there], g_recv.at[c, here], g_ssem.at[0], g_rsem.at[0],
+                    device_id={"blk": peer}, device_id_type=MESH,
+                ).start()
+
+        each_peer(act)
 
     def send_wall(k):
         def act(peer, there, here):
@@ -217,8 +262,10 @@
         )
 
     def store_layer(k, q, layer):
-        field[k % 2, q, pl.ds(8, FP), :] = layer
-        if k < SUB:
+        if k == SUB:
+            fluid_out[q] = layer
+        else:
+            field[k % 2, q, pl.ds(8, FP), :] = layer
             pitch_send[k, 0, pl.ds(q, 1), :] = layer[0:1]
             pitch_send[k, 1, pl.ds(q, 1), :] = layer[FP - 1 : FP]
 
@@ -235,15 +282,25 @@
                 total = total + layer_ends(layer, q)
             return total
 
-        packed[...] = lax.fori_loop(1, FZ, step, jnp.zeros((8, 128), F32))
+        total = lax.fori_loop(1, FZ, step, jnp.zeros((8, 128), F32))
+        if k + 1 < SUB:
+            edge_send[k + 1] = total + layer_ends(base0[...], 0)
+            send_edge(k + 1)
 
     def finish_layer(k):
         take_wall(k)
-        layer = base0[...] + WALL * film[...] * gathered(k)
+        walls = gathered(k, 3 * FP if k + 1 < SUB else FP)
+        layer = base0[...] + WALL * film[...] * walls[0:FP]
         store_layer(k + 1, 0, layer)
         if k + 1 < SUB:
-            edge_send[k + 1] = packed[...] + layer_ends(layer, 0)
-            send_halo(k + 1)
+            send_pitch(k + 1)
+            total = jnp.zeros((8, 128), F32)
+            for t in range(TILES):
+                low = walls[FP + 8 * t : FP + 8 * t + 8]
+                high = walls[2 * FP + 8 * t : 2 * FP + 8 * t + 8]
+                total = jnp.where(lane == 2 * t + 1, roll(low, 2 * t + 2, 1), total)
+                total = jnp.where(lane == 2 * t, roll(high, 2 * t, 1) if t else high, total)
+            edge_fix[...] = edge_film[...] * total
 
     def conduct_of(metal):
         return cond[...] * (1.0 + 0.25 * jnp.tanh(metal))
@@ -279,11 +336,13 @@
 
     def publish(k, metal):
         table[k, 0] = metal[0:1]
+        if k:
+            send_wall(k)
         conduct = conduct_of(metal)
         pack_rim(k, metal, conduct)
         return conduct
 
-    for copy in loads[:4]:
+    for copy in loads[1:5]:
         copy.wait()
     h = film[...]
     v = h * field[0, 0, pl.ds(8, FP), :]
@@ -300,7 +359,9 @@
         return total + layer_ends(layer, q)
 
     edge_send[0] = lax.fori_loop(0, FZ, first_ends, jnp.zeros((8, 128), F32))
-    for copy in loads[4:]:
+    const_send[0] = layer_ends(WALL * h, 0)
+    const_send[1] = jnp.concatenate([jnp.broadcast_to(owner, (8, FP)).astype(F32)] * 2, 1)
+    for copy in loads[5:]:
         copy.wait()
 
     def coefficients(q, carry):
@@ -317,21 +378,22 @@
     def flux_ahead(dest, layer):
         g_send.at[dest].reshape(N_BLK, FS)[...] = placed(film[...] * layer)
 
-    send_halo(0)
-    send_wall(0)
-    send_flux(0, 2, 0)
+    send_pitch(0)
+    send_edge(0)
+    send_const()
     send_rim(0)
+    send_first()
     ends = take_halo(0)
     flux_ahead(2, wall_layer(0, ends))
+    other_layers(0, ends)
     send_flux(2, 2, 1)
-    other_layers(0, ends)
+    take_const()
     calm = metal_step(metal, conduct, take_rim(0))
     finish_layer(0)
     g0, total_h = take_flux(0, 2, 0)
     wall0 = metal[0:1]
     metal = heated(calm, g0 - wall0 * total_h)
     conduct = publish(1, metal)
-    send_wall(1)
     send_rim(1)
     ends = take_halo(1)
     flux_ahead(4, wall_layer(1, ends))
@@ -342,7 +404,6 @@
     g1, total_f = take_flux(2, 2, 1)
     metal = heated(calm, g1 + wall0 * total_f - wall1 * total_h)
     conduct = publish(2, metal)
-    send_wall(2)
     send_rim(2)
     finish_layer(1)
     calm = metal_step(metal, conduct, take_rim(2))
@@ -353,7 +414,6 @@
     (g2,) = take_flux(4, 1, 2)
     metal = heated(calm, g2 + wall1 * total_f - wall2 * total_h)
     conduct = publish(3, metal)
-    send_wall(3)
     send_rim(3)
     other_layers(2, ends)
     finish_layer(2)
@@ -361,20 +421,10 @@
     ends = take_halo(3)
     wall_layer(3, ends)
     other_layers(3, ends)
-    rest = pltpu.make_async_copy(
-        field.at[0, pl.ds(1, FZ - 1), pl.ds(8, FP), :], fluid_out.at[pl.ds(1, FZ - 1)], io_sem.at[0]
-    )
-    rest.start()
     calm = metal_step(metal, conduct, take_rim(3))
     finish_layer(3)
-    last = pltpu.make_async_copy(
-        field.at[0, 0, pl.ds(8, FP), :], fluid_out.at[0], io_sem.at[1]
-    )
-    last.start()
     (g3,) = take_flux(5, 1, 3)
-    solid[...] = heated(calm, g3 + wall2 * total_f - wall3 * total_h)
-    metal_copy = pltpu.make_async_copy(solid, solid_out.at[0], io_sem.at[2])
-    metal_copy.start()
+    solid_out[0] = heated(calm, g3 + wall2 * total_f - wall3 * total_h)
 
     for first, count, sem in ((0, 2, 0), (2, 2, 1), (4, 1, 2), (5, 1, 3)):
         sent = g_send.at[pl.ds(first, count), pl.ds(1, N_BLK - 1)]
@@ -389,24 +439,34 @@
             pltpu.make_async_copy(sent, sent, h_ssem.at[k, 2 + i]).wait()
             sent = rim_send.at[k]
             pltpu.make_async_copy(sent, sent, r_ssem.at[k, i]).wait()
-    rest.wait()
-    last.wait()
-    metal_copy.wait()
+    for i in range(2):
+        pltpu.make_async_copy(const_send, const_send, c_ssem.at[i]).wait()
+
+
+def write_out(fluid, metal, fluid_out, metal_out, sem):
+    copies = [
+        pltpu.make_async_copy(fluid, fluid_out, sem.at[0]),
+        pltpu.make_async_copy(metal, metal_out, sem.at[1]),
+    ]
+    for copy in copies:
+        copy.start()
+    for copy in copies:
+        copy.wait()
 
 
 def local(
     fluid_temp, stream_velocity, pitch_velocity, film_coeff, solid_temp, conductivity, face_owner
 ):
     dma = pltpu.SemaphoreType.DMA
-    anywhere = pl.BlockSpec(memory_space=pl.ANY)
-    return pl.pallas_call(
+    anywhere = pl.BlockSpec(memory_space=pltpu.HBM)
+    fluid, metal = pl.pallas_call(
         kernel,
         out_shape=(
             jax.ShapeDtypeStruct((FZ, FP, FS), F32),
             jax.ShapeDtypeStruct((1, SD, FS), F32),
         ),
-        in_specs=[anywhere] * 6 + [pl.BlockSpec(memory_space=pltpu.VMEM)],
-        out_specs=(anywhere, anywhere),
+        in_specs=[anywhere] * 7,
+        out_specs=[pl.BlockSpec(memory_space=pltpu.VMEM)] * 2,
         scratch_shapes=[
             pltpu.VMEM((2, FZ, FP + 16, FS), F32),
             pltpu.VMEM((2, FZ, FP, FS), F32),
@@ -414,9 +474,13 @@
             pltpu.VMEM((FP, FS), F32),
             pltpu.VMEM((SD, FS), F32),
             pltpu.VMEM((SD, FS), F32),
-            pltpu.VMEM((FP, N_BLK), F32),
-            pltpu.VMEM((N_BLK, FP), F32),
+            pltpu.VMEM((1, FP), jnp.int32),
+            pltpu.VMEM((3 * FP, N_BLK), BF16),
+            pltpu.VMEM((N_BLK, FP), BF16),
             pltpu.VMEM((FP, FS), F32),
+            pltpu.VMEM((2, 8, FS), F32),
+            pltpu.VMEM((2, 2, 8, FS), F32),
+            pltpu.VMEM((8, FS), F32),
             pltpu.VMEM((8, FS), F32),
             pltpu.VMEM((6, N_BLK, 1, FS), F32),
             pltpu.VMEM((6, N_BLK, 1, FS), F32),
@@ -427,11 +491,32 @@
             pltpu.VMEM((SUB, 2, 8, FS), F32),
             pltpu.VMEM((SUB, 8, FS), F32),
             pltpu.VMEM((SUB, 2, 8, FS), F32),
-            dma((6,)), dma((4,)), dma((4,)), dma((SUB,)), dma((SUB,)),
-            dma((SUB, 4)), dma((SUB, 4)), dma((SUB, 2)), dma((SUB, 2)),
+            dma((7,)), dma((4,)), dma((4,)), dma((SUB,)), dma((SUB,)),
+            dma((SUB, 4)), dma((SUB, 4)), dma((SUB, 2)), dma((SUB, 2)), dma((2,)), dma((2,)),
         ],
-        compiler_params=pltpu.CompilerParams(collective_id=0, has_side_effects=True),
-    )(fluid_temp, stream_velocity, pitch_velocity, film_coeff, solid_temp, conductivity, face_owner)
+        compiler_params=pltpu.CompilerParams(
+            collective_id=0, has_side_effects=True, vmem_limit_bytes=16 << 20
+        ),
+    )(
+        *(
+            pltpu.with_memory_space_constraint(array, pltpu.HBM)
+            for array in (
+                fluid_temp, stream_velocity, pitch_velocity, film_coeff, solid_temp, conductivity,
+                face_owner.reshape(1, FP),
+            )
+        )
+    )
+    return pl.pallas_call(
+        write_out,
+        out_shape=(
+            jax.ShapeDtypeStruct((FZ, FP, FS), F32),
+            jax.ShapeDtypeStruct((1, SD, FS), F32),
+        ),
+        in_specs=[pl.BlockSpec(memory_space=pltpu.VMEM)] * 2,
+        out_specs=[anywhere] * 2,
+        scratch_shapes=[dma((2,))],
+        compiler_params=pltpu.CompilerParams(vmem_limit_bytes=1 << 20),
+    )(fluid, metal)
 
 
 def solution(mesh):

time: 69.2 us -> 62.7 us (0.906)
  local copies, waits for them, and re-layouts: 3.64 us -> 0 us
  Pallas kernels: 64.7 us -> 61.9 us
    unnamed x5 -> x0, local copies, waits for them, and re-layouts: 3.64 us -> none
    pallas_call x1, Pallas kernels: 64.7 us -> 61.2 us  [local(): pl.pallas_call(kernel, out_shape=(jax.ShapeDtypeStruct((FZ, FP, FS), F32)...]
    pallas_call x0 -> x1, Pallas kernels: none -> 0.72 us  [local(): pl.pallas_call(write_out, out_shape=(jax.ShapeDtypeStruct((FZ, FP, FS), F...]
where the time goes in v2:
time: 62.7 us; the launch traced here: 62.6 us
  Pallas kernels  61.9 us (99%)
  between operations  0.64 us (1%)
    pallas_call x1, Pallas kernels, local(): pl.pallas_call(kernel, out_shape=(jax.ShapeDtypeStruct((FZ, FP, FS), F32)...  61.2 us

profile of v2, /device:TPU:8, one launch (start us, length us, event | category | flops | bytes accessed | tf_op | source)
XLA Modules:
  0.0 62.6 jit_solution(11154841824075110811)
XLA Ops:
  0.6 61.2 %shard_map.86 = (f32[8,64,128]{2,1,0:T(8,128)S(1)}, f32[1,32,128]{2,1,0:T(8,128)S(1)}) custom-call(f32[8,64,128]{2,1,0:T(8,128)} %fluid_in.1, f32[8,64,128]{2,1,0:T(8,128)} %stream_in.1, f32[8,64,128]{2,1,0:T(8,128)} %pitch_in.1, f32[64,128]{1,0:T(8,128)} %film_in.1, f32[1,32,128]{2,1,0:T(8,128)} %solid_in.1, f32[1,32,128]{2,1,0:T(8,128)} %cond_in.1, ...), custom_call_target="tpu_custom_call" | custom-call | tf_op jit(solution)/shard_map/pallas_call | solution.py:462
  61.9 0.7 %shard_map.87 = (f32[8,64,128]{2,1,0:T(8,128)}, f32[1,32,128]{2,1,0:T(8,128)}) custom-call(f32[8,64,128]{2,1,0:T(8,128)S(1)} %get-tuple-element.4.fluid, f32[1,32,128]{2,1,0:T(8,128)S(1)} %get-tuple-element.5.metal), custom_call_target="tpu_custom_call" | custom-call | tf_op jit(solution)/shard_map/pallas_call | solution.py:509

commit v3 on v2

--- a/solution.py
+++ b/solution.py
@@ -336,7 +336,7 @@
 
     def publish(k, metal):
         table[k, 0] = metal[0:1]
-        if k:
+        if k % 2:
             send_wall(k)
         conduct = conduct_of(metal)
         pack_rim(k, metal, conduct)
@@ -406,15 +406,16 @@
     conduct = publish(2, metal)
     send_rim(2)
     finish_layer(1)
+    send_wall(2)
     calm = metal_step(metal, conduct, take_rim(2))
     wall2 = metal[0:1]
-    ends = take_halo(2)
-    flux_ahead(5, wall_layer(2, ends))
-    send_flux(5, 1, 3)
     (g2,) = take_flux(4, 1, 2)
     metal = heated(calm, g2 + wall1 * total_f - wall2 * total_h)
     conduct = publish(3, metal)
     send_rim(3)
+    ends = take_halo(2)
+    flux_ahead(5, wall_layer(2, ends))
+    send_flux(5, 1, 3)
     other_layers(2, ends)
     finish_layer(2)
     wall3 = metal[0:1]

time: 62.7 us -> 61.9 us (0.987)
  Pallas kernels: 61.9 us -> 61.1 us
    pallas_call x1, Pallas kernels: 61.2 us -> 60.4 us  [local(): pl.pallas_call(kernel, out_shape=(jax.ShapeDtypeStruct((FZ, FP, FS), F32)...]
where the time goes in v3:
time: 61.9 us; the launch traced here: 61.7 us
  Pallas kernels  61.1 us (99%)
  between operations  0.64 us (1%)
    pallas_call x1, Pallas kernels, local(): pl.pallas_call(kernel, out_shape=(jax.ShapeDtypeStruct((FZ, FP, FS), F32)...  60.4 us

profile of v3, /device:TPU:8, one launch (start us, length us, event | category | flops | bytes accessed | tf_op | source)
XLA Modules:
  0.0 61.7 jit_solution(9562894963336590697)
XLA Ops:
  0.6 60.4 %shard_map.86 = (f32[8,64,128]{2,1,0:T(8,128)S(1)}, f32[1,32,128]{2,1,0:T(8,128)S(1)}) custom-call(f32[8,64,128]{2,1,0:T(8,128)} %fluid_in.1, f32[8,64,128]{2,1,0:T(8,128)} %stream_in.1, f32[8,64,128]{2,1,0:T(8,128)} %pitch_in.1, f32[64,128]{1,0:T(8,128)} %film_in.1, f32[1,32,128]{2,1,0:T(8,128)} %solid_in.1, f32[1,32,128]{2,1,0:T(8,128)} %cond_in.1, ...), custom_call_target="tpu_custom_call" | custom-call | tf_op jit(solution)/shard_map/pallas_call | solution.py:463
  61.0 0.7 %shard_map.87 = (f32[8,64,128]{2,1,0:T(8,128)}, f32[1,32,128]{2,1,0:T(8,128)}) custom-call(f32[8,64,128]{2,1,0:T(8,128)S(1)} %get-tuple-element.4.fluid, f32[1,32,128]{2,1,0:T(8,128)S(1)} %get-tuple-element.5.metal), custom_call_target="tpu_custom_call" | custom-call | tf_op jit(solution)/shard_map/pallas_call | solution.py:510
